TPU v7x, 32 devices: a whole 2x2x4 slice. The times are simulated.
32 devices in a mesh: row: 8 (over y, x, core), col: 4 (over z).
Axes of the slice: x: 2, y: 2, z: 4, core: 2. Of those that a mesh axis runs over, the one named last changes fastest.
Arguments:
- coeffs: bfloat16 [6144, 4096], P('row', 'col'), may hold values from -0.00390625 to 0.00390625
- occupation: float32 [4096], P('col'), may hold values from 0.5 to 2
- basis_on_grid: bfloat16 [320, 512, 512], P('row'), may hold values from -6 to 6
- basis_map: int32 [320, 512], P('row'), may hold values from 0 to 6143, as said below
- basis_count: int32 [320], P('row'), may hold values from 256 to 512
- batch_atom: int32 [320], P('row'), may hold values from 0 to 63
- harmonics: float32 [320, 49, 512], P('row'), may hold values from -0.25 to 0.25
Outputs:
- density: float32 [320, 512], P('row', 'col')
- moments: float32 [64, 49], replicated
Inputs may be any that keep to these rules, and one draw needn't show every extreme that they name: `basis_map`: the slots of one batch name distinct basis functions. With R = 768 and o = b // 40, batch b names only basis functions q * R + (o * 96 + w) mod R with 0 <= q < 8 and 0 <= w < 96.
All inputs are finite; a program needn't handle non-finite values.
Results may differ from a plain program's by a relative error of at most 0.0003.
Values may be sent and summed in bfloat16 or wider, within the bound.
No kernel may reach another device: no remote copies, remote signals or barrier semaphores. Data moves between devices by JAX's collectives and lax.ppermute only.
A program may use at most 192 MiB of HBM per device.

v0:
```python
import jax
import jax.numpy as jnp
from jax import lax
from jax.sharding import PartitionSpec as P

WIN = 96
NATOM = 64


def shards(coeffs, occupation, basis_on_grid, basis_map, basis_count, batch_atom, harmonics):
    batches, points, slots = basis_on_grid.shape
    owned = coeffs.shape[0]
    owners = lax.axis_size("row")
    target = lax.broadcasted_iota(jnp.int32, (owners, WIN), 0)
    offset = lax.broadcasted_iota(jnp.int32, (owners, WIN), 1)
    outgoing_ids = jnp.mod(target * WIN + offset, owned).reshape(-1)
    outgoing = jnp.take(coeffs, outgoing_ids, axis=0)
    window = lax.all_to_all(outgoing, "row", split_axis=0, concat_axis=0, tiled=True)
    start = jnp.mod(lax.axis_index("row") * WIN, owned)
    source = basis_map // owned
    within = jnp.mod(basis_map % owned - start, owned)
    local_ids = source * WIN + within
    selected = jnp.take(window, local_ids, axis=0)
    slot_ids = lax.broadcasted_iota(jnp.int32, (batches, slots), 1)
    keep = slot_ids < basis_count[:, None]
    masked = jnp.where(keep[:, None, :], basis_on_grid, jnp.zeros_like(basis_on_grid))
    orbital = jnp.einsum("bps,bsk->bpk", masked, selected, preferred_element_type=jnp.float32)
    partial_density = jnp.sum(orbital * orbital * occupation[None, None, :], axis=2)
    atom_ids = lax.broadcasted_iota(jnp.int32, (batches, NATOM), 1)
    member = (batch_atom[:, None] == atom_ids).astype(jnp.float32)
    full_density = lax.psum(partial_density, "col")
    local_moment = jnp.einsum(
        "blp,bp->bl", harmonics, full_density, precision=lax.Precision.HIGHEST
    )
    atom_part = jnp.dot(member.T, local_moment, precision=lax.Precision.HIGHEST)
    moments = lax.psum(atom_part, "row")
    share = points // lax.axis_size("col")
    density = lax.dynamic_slice_in_dim(full_density, lax.axis_index("col") * share, share, 1)
    return (density, moments)


def solution(mesh):
    placed = (
        P("row", "col"),
        P("col"),
        P("row", None, None),
        P("row", None),
        P("row"),
        P("row"),
        P("row", None, None),
    )
    return jax.shard_map(
        shards, mesh=mesh, in_specs=placed, out_specs=(P("row", "col"), P()), check_vma=False
    )
```

profile of v0, /device:TPU:0, one launch (start us, length us, event | category | flops | bytes accessed | tf_op | source)
XLA Modules:
  0.0 228.4 jit_solution(9429908495071229577)
XLA Ops:
  7.2 0.0 copy-start
  7.2 0.1 add_remainder_fusion
  7.3 0.1 compare_and_fusion.1
  7.4 0.1 rem.52
  7.5 1.1 copy-done
  8.6 2.8 %gather_fusion = bf16[768,1024]{1,0:T(8,128)(2,1)S(1)} fusion(bf16[768,1024]{1,0:T(8,128)(2,1)S(1)} %copy-done, s32[1024]{0:T(1024)S(1)} %pad_clamp_fusion), kind=kCustom, calls=%fused_computation | custom fusion | bytes 3148800 | tf_op jit(solution)/shard_map/jit(_take)/gather | solution.py:17
  11.4 1.4 broadcast_select_fusion
  12.8 5.2 %all-to-all-start = ((bf16[8,96,1024]{2,1,0:T(8,128)(2,1)}), bf16[8,96,1024]{2,1,0:T(8,128)(2,1)S(1)}, u32[]{:S(2)}, u32[]{:S(2)}) async-start(bf16[8,96,1024]{2,1,0:T(8,128)(2,1)} %broadcast_select_fusion), calls=%async_computation | async-start | bytes 3145728 | tf_op jit(solution)/shard_map/all_to_all | solution.py:18
  18.0 0.0 all-reduce.2.cloned.1.call-start
  18.0 1.0 compare_and_fusion
  19.1 0.7 iota_compare_fusion
  19.9 19.1 %all-to-all-done = bf16[8,96,1024]{2,1,0:T(8,128)(2,1)S(1)} async-done(((bf16[8,96,1024]{2,1,0:T(8,128)(2,1)}), bf16[8,96,1024]{2,1,0:T(8,128)(2,1)S(1)}, u32[]{:S(2)}, u32[]{:S(2)}) %all-to-all-start) | async-done | bytes 1572896 | tf_op jit(solution)/shard_map/all_to_all | solution.py:18
  39.0 0.0 copy-start.2
  39.0 87.0 %gather_fusion.1 = bf16[20480,1024]{1,0:T(8,128)(2,1)} fusion(bf16[768,1024]{1,0:T(8,128)(2,1)S(1)} %bitcast.9, s32[20480]{0:T(1024)S(1)} %broadcast_clamp_fusion), kind=kCustom, calls=%fused_computation.1 | custom fusion | bytes 83968000 | tf_op jit(solution)/shard_map/jit(_take)/gather | solution.py:23
  125.9 0.0 copy-done.2
  125.9 0.0 copy-start.3
  125.9 0.0 copy-start.1
  125.9 29.3 %multiply_reduce_fusion = f32[40,512]{1,0:T(8,128)} fusion(f32[1024]{0:T(1024)S(1)} %copy-done.2, bf16[40,512,1024]{2,1,0:T(8,128)(2,1)} %bitcast.10, pred[40,512]{1,0:T(8,128)(4,1)S(1)} %get-tuple-element.2, bf16[40,512,512]{2,1,0:T(8,128)(2,1)} %param.9, pred[40,512]{1,0:T(8,128)(4,1)S(1)} %iota_compare_fusion), kind=kOutput, calls=%fused_computation.2 | convolution fusion | flops 21569187840 | bytes 63041536 | tf_op jit(solution)/shard_map/bps,bsk->bpk/dot_general | solution.py:27
  155.2 0.0 all-reduce.2.cloned.1.call-update
  155.3 33.8 %all-reduce.2.cloned.1.call-done = f32[40,512]{1,0:T(8,128)} async-done(((f32[40,512]{1,0:T(8,128)}), f32[40,512]{1,0:T(8,128)}) %all-reduce.2.cloned.1.call-update) | async-done | bytes 81936 | tf_op jit(solution)/shard_map/psum | solution.py:31
  189.0 7.9 %fusion.11 = f32[40,1,49]{2,1,0:T(1,128)S(1)} fusion(f32[40,49,512]{2,0,1:T(8,128)} %param.13, f32[40,512,1]{1,0,2:T(8,128)} %bitcast.14), kind=kOutput, calls=%fused_computation.10 | convolution fusion | flops 12042240 | bytes 4103840 | tf_op jit(solution)/shard_map/blp,bp->bl/dot_general | solution.py:32
  196.9 0.0 copy-done.3
  196.9 0.2 fusion.19
  197.2 23.0 %psum.15 = f32[64,49]{0,1:T(8,128)} all-reduce(f32[64,49]{0,1:T(8,128)S(1)} %fusion.19), channel_id=1, replica_groups=mesh['row'=8,'col'=4] {'row'}, use_global_device_ids=true, to_apply=%region_2.3 | all-reduce | flops 3136 | bytes 25088 | tf_op jit(solution)/shard_map/psum | solution.py:36
  220.2 1.3 constant_dynamic-slice_fusion
  221.5 0.0 copy-done.1
  (5 shorter events, 0.1 us)
Async XLA Ops:
  7.2 1.4 copy-start
  12.8 26.2 %all-to-all-start = ((bf16[8,96,1024]{2,1,0:T(8,128)(2,1)}), bf16[8,96,1024]{2,1,0:T(8,128)(2,1)S(1)}, u32[]{:S(2)}, u32[]{:S(2)}) async-start(bf16[8,96,1024]{2,1,0:T(8,128)(2,1)} %broadcast_select_fusion), calls=%async_computation | async-start | bytes 3145728 | tf_op jit(solution)/shard_map/all_to_all | solution.py:18
  18.0 171.1 %all-reduce.2.cloned.1.call-start = ((), (), s32[]{:S(2)}) async-start(), calls=%async_computation.1 | async-start | bytes 163840 | tf_op jit(solution)/shard_map/psum | solution.py:31
  39.0 87.0 %copy-start.2 = (f32[1024]{0:T(1024)S(1)}, f32[1024]{0:T(1024)}, u32[]{:S(2)}) copy-start(f32[1024]{0:T(1024)} %param.8) | copy-start | bytes 12292
  125.9 71.0 %copy-start.3 = (s32[40]{0:T(128)S(1)}, s32[40]{0:T(128)}, u32[]{:S(2)}) copy-start(s32[40]{0:T(128)} %param.12) | copy-start | bytes 484
  125.9 95.6 %copy-start.1 = (bf16[768,1024]{1,0:T(8,128)(2,1)S(1)}, bf16[768,1024]{1,0:T(8,128)(2,1)}, u32[]{:S(2)}) copy-start(bf16[768,1024]{1,0:T(8,128)(2,1)} %param.7) | copy-start | bytes 4718596
Sparse Core Ops, SparseCore 0:
  155.4 33.6 all-reduce.1
where the time goes:
time: 229 us; the launch traced here: 228 us
  local copies, waits for them, and re-layouts  92.3 us (40%)
  waiting for transfers between devices  52.9 us (23%)
  matrix products  37.5 us (16%)
  blocking collectives  23 us (10%)
  between operations  14.1 us (6%)
  starting transfers between devices  5.24 us (2%)
  other arithmetic  3.37 us (1%)
    gather x1, local copies, waits for them, and re-layouts, shards(): selected = jnp.take(window, local_ids, axis=0)  87 us
    psum x1, waiting for transfers between devices, shards(): full_density = lax.psum(partial_density, 'col')  33.8 us
    dot_general x1, matrix products, shards(): jnp.einsum('bps,bsk->bpk', masked, selected, preferred_element_type=jnp.f...  29.3 us
    psum x1, blocking collectives, shards(): moments = lax.psum(atom_part, 'row')  23 us
    all_to_all x1, waiting for transfers between devices, shards(): lax.all_to_all(outgoing, 'row', split_axis=0, concat_axis=0, tiled=True)  19.1 us
    dot_general x1, matrix products, shards(): jnp.einsum('blp,bp->bl', harmonics, full_density, precision=lax.Precision...  7.89 us
    all_to_all x1, starting transfers between devices, shards(): lax.all_to_all(outgoing, 'row', split_axis=0, concat_axis=0, tiled=True)  5.2 us
  transfers between devices with their start and end apart: 2, of which 2 were waited for; matrix products, arithmetic and copies ran while one was open for 1% of the time, Pallas kernels for 0%

commit v1 on v0

--- a/solution.py
+++ b/solution.py
@@ -28,7 +28,11 @@
     partial_density = jnp.sum(orbital * orbital * occupation[None, None, :], axis=2)
     atom_ids = lax.broadcasted_iota(jnp.int32, (batches, NATOM), 1)
     member = (batch_atom[:, None] == atom_ids).astype(jnp.float32)
-    full_density = lax.psum(partial_density, "col")
+    full_density = partial_density
+    for hop in (1, 2):
+        full_density = full_density + lax.ppermute(
+            full_density, "col", [(dev, dev ^ hop) for dev in range(4)]
+        )
     local_moment = jnp.einsum(
         "blp,bp->bl", harmonics, full_density, precision=lax.Precision.HIGHEST
     )

time: 229 us -> 192 us (0.84)
  waiting for transfers between devices: 52.9 us -> 27.2 us
  between operations: 14.1 us -> 0.71 us
  starting transfers between devices: 5.24 us -> 8.86 us
    psum x1 -> x0, waiting for transfers between devices: 33.8 us -> none  [shards(): full_density = lax.psum(partial_density, 'col')]
    ppermute x0 -> x2, waiting for transfers between devices: none -> 8 us  [shards(): lax.ppermute(full_density, 'col', [(dev, dev ^ hop) for dev in range(4)])]
    ppermute x0 -> x2, starting transfers between devices: none -> 3.67 us  [shards(): lax.ppermute(full_density, 'col', [(dev, dev ^ hop) for dev in range(4)])]
  transfers between devices with their start and end apart: 2 -> 3, of which waited for: 2 -> 3; matrix products, arithmetic and copies ran while one was open for 1% -> 1% of each run, Pallas kernels for 0% -> 0%
where the time goes in v1:
time: 192 us
  local copies, waits for them, and re-layouts  91.9 us (48%)
  matrix products  36.7 us (19%)
  waiting for transfers between devices  27.2 us (14%)
  blocking collectives  23 us (12%)
  starting transfers between devices  8.86 us (5%)
  other arithmetic  3.4 us (2%)
    gather x1, local copies, waits for them, and re-layouts, shards(): selected = jnp.take(window, local_ids, axis=0)  87.3 us
    dot_general x1, matrix products, shards(): jnp.einsum('bps,bsk->bpk', masked, selected, preferred_element_type=jnp.f...  28.6 us
    psum x1, blocking collectives, shards(): moments = lax.psum(atom_part, 'row')  23 us
    all_to_all x1, waiting for transfers between devices, shards(): lax.all_to_all(outgoing, 'row', split_axis=0, concat_axis=0, tiled=True)  19.2 us
    ppermute x2, waiting for transfers between devices, shards(): lax.ppermute(full_density, 'col', [(dev, dev ^ hop) for dev in range(4)])  8 us
    dot_general x1, matrix products, shards(): jnp.einsum('blp,bp->bl', harmonics, full_density, precision=lax.Precision...  7.84 us
    all_to_all x1, starting transfers between devices, shards(): lax.all_to_all(outgoing, 'row', split_axis=0, concat_axis=0, tiled=True)  5.2 us
  transfers between devices with their start and end apart: 3, of which 3 were waited for; matrix products, arithmetic and copies ran while one was open for 1% of the time, Pallas kernels for 0%

profile of v1, /device:TPU:0, one launch (start us, length us, event | category | flops | bytes accessed | tf_op | source)
XLA Modules:
  0.0 191.8 jit_solution(6720098487561837298)
XLA Ops:
  0.6 0.0 copy-start
  0.7 0.1 add_remainder_fusion
  0.7 0.1 compare_and_fusion.1
  0.8 0.1 rem.52
  0.9 1.1 copy-done
  2.0 2.8 %gather_fusion = bf16[768,1024]{1,0:T(8,128)(2,1)S(1)} fusion(bf16[768,1024]{1,0:T(8,128)(2,1)S(1)} %copy-done, s32[1024]{0:T(1024)S(1)} %pad_clamp_fusion), kind=kCustom, calls=%fused_computation | custom fusion | bytes 3148800 | tf_op jit(solution)/shard_map/jit(_take)/gather | solution.py:17
  4.9 1.4 broadcast_select_fusion
  6.2 5.2 %all-to-all-start = ((bf16[8,96,1024]{2,1,0:T(8,128)(2,1)}), bf16[8,96,1024]{2,1,0:T(8,128)(2,1)S(1)}, u32[]{:S(2)}, u32[]{:S(2)}) async-start(bf16[8,96,1024]{2,1,0:T(8,128)(2,1)} %broadcast_select_fusion), calls=%async_computation | async-start | bytes 3145728 | tf_op jit(solution)/shard_map/all_to_all | solution.py:18
  11.4 1.0 compare_and_fusion
  12.5 0.7 iota_compare_fusion
  13.3 19.2 %all-to-all-done = bf16[8,96,1024]{2,1,0:T(8,128)(2,1)S(1)} async-done(((bf16[8,96,1024]{2,1,0:T(8,128)(2,1)}), bf16[8,96,1024]{2,1,0:T(8,128)(2,1)S(1)}, u32[]{:S(2)}, u32[]{:S(2)}) %all-to-all-start) | async-done | bytes 1572896 | tf_op jit(solution)/shard_map/all_to_all | solution.py:18
  32.4 0.0 copy-start.2
  32.4 87.3 %gather_fusion.1 = bf16[20480,1024]{1,0:T(8,128)(2,1)} fusion(bf16[768,1024]{1,0:T(8,128)(2,1)S(1)} %bitcast.9, s32[20480]{0:T(1024)S(1)} %broadcast_clamp_fusion), kind=kCustom, calls=%fused_computation.1 | custom fusion | bytes 83968000 | tf_op jit(solution)/shard_map/jit(_take)/gather | solution.py:23
  119.7 0.0 copy-done.2
  119.7 0.0 copy-start.3
  119.7 0.0 copy-start.1
  119.7 28.6 %multiply_reduce_fusion = f32[40,512]{1,0:T(8,128)S(1)} fusion(f32[1024]{0:T(1024)S(1)} %copy-done.2, bf16[40,512,1024]{2,1,0:T(8,128)(2,1)} %bitcast.10, pred[40,512]{1,0:T(8,128)(4,1)S(1)} %get-tuple-element.2, bf16[40,512,512]{2,1,0:T(8,128)(2,1)} %param.9, pred[40,512]{1,0:T(8,128)(4,1)S(1)} %iota_compare_fusion), kind=kOutput, calls=%fused_computation.2 | convolution fusion | flops 21569187840 | bytes 63041536 | tf_op jit(solution)/shard_map/bps,bsk->bpk/dot_general | solution.py:27
  148.4 1.6 collective-permute-start
  150.0 3.7 %collective-permute-done = f32[40,512]{1,0:T(8,128)S(1)} collective-permute-done((f32[40,512]{1,0:T(8,128)S(1)}, f32[40,512]{1,0:T(8,128)S(1)}, u32[]{:S(2)}, u32[]{:S(2)}) %collective-permute-start) | collective-permute-done | bytes 81952 | tf_op jit(solution)/shard_map/ppermute | solution.py:33
  153.8 2.0 %collective-permute-start.1 = (f32[40,512]{1,0:T(8,128)S(1)}, f32[40,512]{1,0:T(8,128)S(1)}, u32[]{:S(2)}, u32[]{:S(2)}) collective-permute-start(f32[40,512]{1,0:T(8,128)S(1)} %add.99), channel_id=1, source_target_pairs={{0,2},{1,3},{2,0},{3,1},{4,6},{5,7},{6,4},{7,5},{8,10},{9,11},{10,... | collective-permute-start | bytes 245768 | tf_op jit(solution)/shard_map/ppermute | solution.py:33
  155.8 4.3 %collective-permute-done.1 = f32[40,512]{1,0:T(8,128)S(1)} collective-permute-done((f32[40,512]{1,0:T(8,128)S(1)}, f32[40,512]{1,0:T(8,128)S(1)}, u32[]{:S(2)}, u32[]{:S(2)}) %collective-permute-start.1) | collective-permute-done | bytes 81952 | tf_op jit(solution)/shard_map/ppermute | solution.py:33
  160.1 7.8 %fusion.11 = f32[40,1,49]{2,1,0:T(1,128)S(1)} fusion(f32[40,49,512]{2,0,1:T(8,128)} %param.13, f32[40,512,1]{1,0,2:T(8,128)S(1)} %bitcast.12), kind=kOutput, calls=%fused_computation.10 | convolution fusion | flops 12042240 | bytes 4103840 | tf_op jit(solution)/shard_map/blp,bp->bl/dot_general | solution.py:36
  167.9 0.0 copy-done.3
  167.9 0.2 fusion.19
  168.2 23.0 %psum.7 = f32[64,49]{0,1:T(8,128)} all-reduce(f32[64,49]{0,1:T(8,128)S(1)} %fusion.19), channel_id=1, replica_groups=mesh['row'=8,'col'=4] {'row'}, use_global_device_ids=true, to_apply=%region_1.2 | all-reduce | flops 3136 | bytes 25088 | tf_op jit(solution)/shard_map/psum | solution.py:40
  191.1 0.6 constant_dynamic-slice_fusion
  191.8 0.0 copy-done.1
  (7 shorter events, 0.1 us)
Async XLA Ops:
  0.6 1.4 copy-start
  6.2 26.2 %all-to-all-start = ((bf16[8,96,1024]{2,1,0:T(8,128)(2,1)}), bf16[8,96,1024]{2,1,0:T(8,128)(2,1)S(1)}, u32[]{:S(2)}, u32[]{:S(2)}) async-start(bf16[8,96,1024]{2,1,0:T(8,128)(2,1)} %broadcast_select_fusion), calls=%async_computation | async-start | bytes 3145728 | tf_op jit(solution)/shard_map/all_to_all | solution.py:18
  32.4 87.3 %copy-start.2 = (f32[1024]{0:T(1024)S(1)}, f32[1024]{0:T(1024)}, u32[]{:S(2)}) copy-start(f32[1024]{0:T(1024)} %param.8) | copy-start | bytes 12292
  119.7 48.2 %copy-start.3 = (s32[40]{0:T(128)S(1)}, s32[40]{0:T(128)}, u32[]{:S(2)}) copy-start(s32[40]{0:T(128)} %param.12) | copy-start | bytes 484
  119.7 72.1 %copy-start.1 = (bf16[768,1024]{1,0:T(8,128)(2,1)S(1)}, bf16[768,1024]{1,0:T(8,128)(2,1)}, u32[]{:S(2)}) copy-start(bf16[768,1024]{1,0:T(8,128)(2,1)} %param.7) | copy-start | bytes 4718596
  148.4 5.4 %collective-permute-start = (f32[40,512]{1,0:T(8,128)S(1)}, f32[40,512]{1,0:T(8,128)S(1)}, u32[]{:S(2)}, u32[]{:S(2)}) collective-permute-start(f32[40,512]{1,0:T(8,128)S(1)} %multiply_reduce_fusion), channel_id=1, source_target_pairs={{0,1},{1,0},{2,3},{3,2},{4,5},{5,4},{6,7},{7,6},{8,9},{9,8},{10,11... | collective-permute-start | bytes 245768 | tf_op jit(solution)/shard_map/ppermute | solution.py:33
  153.8 6.3 %collective-permute-start.1 = (f32[40,512]{1,0:T(8,128)S(1)}, f32[40,512]{1,0:T(8,128)S(1)}, u32[]{:S(2)}, u32[]{:S(2)}) collective-permute-start(f32[40,512]{1,0:T(8,128)S(1)} %add.99), channel_id=1, source_target_pairs={{0,2},{1,3},{2,0},{3,1},{4,6},{5,7},{6,4},{7,5},{8,10},{9,11},{10,... | collective-permute-start | bytes 245768 | tf_op jit(solution)/shard_map/ppermute | solution.py:33
